TPU v7x, 512 devices: a whole 4x8x8 slice. The times are simulated.
512 devices in a mesh: seq: 64 (over x, y, core), head: 8 (over z).
Axes of the slice: x: 4, y: 8, z: 8, core: 2. Of those that a mesh axis runs over, the one named last changes fastest.
Arguments:
- query_feat: bfloat16 [32768, 512], P('seq', 'head'), may hold values from -6 to 6
- key_feat: bfloat16 [32768, 512], P('seq', 'head'), may hold values from -6 to 6
- values: bfloat16 [32768, 4096], P('seq', 'head'), may hold values from -6 to 6
- conv_query: float32 [3, 512], P(None, 'head'), may hold values from -3 to 3
- conv_key: float32 [3, 512], P(None, 'head'), may hold values from -3 to 3
- conv_value: float32 [3, 4096], P(None, 'head'), may hold values from -3 to 3
- norm_gain: float32 [4096], P('head'), may hold values from 0.1 to 1.9
- out_weight: bfloat16 [4096, 4096], P('head', 'seq'), may hold values from -0.09375 to 0.09375
- stream_ids: int32 [64], replicated, may hold values from 0 to 7, never falling along the last dimension, each value on 1 to 32 neighbouring positions
Outputs:
- mixed: bfloat16 [32768, 4096], P('seq', 'head')
Inputs may be any that keep to these rules, and one draw needn't show every extreme that they name: `stream_ids`: stream ids never fall along the shards; each stream holds 1 to 32 consecutive shards, and one stream holds exactly 32.
All inputs are finite; a program needn't handle non-finite values.
Results may differ from a plain program's by a relative error of at most 0.018.
Values may be sent and summed in bfloat16 or wider, within the bound.
A program may use at most 128 MiB of HBM per device.

v0:
```python
import jax
import jax.numpy as jnp
from jax import lax
from jax.sharding import PartitionSpec as P

HD = 128
FEAT = 16
TAYLOR = 273


def from_behind(block, axis, distance):
    devices = range(lax.axis_size(axis))
    route = [(i - distance, i) for i in devices if i - distance in devices]
    return lax.ppermute(block, axis, route)


def entering(value, axis, join, neutral):
    count, mine = (lax.axis_size(axis), lax.axis_index(axis))
    pieces = jax.tree.map(lambda part: lax.all_gather(part, axis), value)
    so_far = jax.tree.map(
        lambda part, zero: jnp.full_like(part, 0) + jnp.asarray(zero, part.dtype), value, neutral
    )

    def lap(position, so_far):
        longer = join(so_far, jax.tree.map(lambda part: part[position], pieces))
        return jax.tree.map(lambda new, old: jnp.where(position < mine, new, old), longer, so_far)

    return lax.fori_loop(0, count - 1, lap, so_far)


def taylor(feats):
    scaled = feats * FEAT ** (-0.25)
    outer = (scaled[..., :, None] * scaled[..., None, :]).reshape(
        scaled.shape[:-1] + (FEAT * FEAT,)
    ) * 0.5**0.5
    ones = jnp.ones(scaled.shape[:-1] + (1,), jnp.float32)
    return jnp.concatenate([ones, scaled, outer], axis=-1)


def convolve(inputs, rim_rows, kernel, keep):
    padded = jnp.concatenate(
        [rim_rows.astype(jnp.float32) * keep, inputs.astype(jnp.float32)], axis=0
    )
    return (kernel[0] * padded[:-2] + kernel[1] * padded[1:-1] + kernel[2] * padded[2:]).astype(
        jnp.bfloat16
    )


def segment_combine(earlier, later):
    return (jnp.maximum(earlier[0], later[0]), later[1] + (1.0 - later[0]) * earlier[1])


def on_device(
    query_feat,
    key_feat,
    values,
    conv_query,
    conv_key,
    conv_value,
    norm_gain,
    out_weight,
    stream_ids,
):
    rows = query_feat.shape[0]
    heads = values.shape[1] // HD
    position = lax.axis_index("seq")
    own_stream = stream_ids[position]
    prior_stream = stream_ids[jnp.maximum(position - 1, 0)]
    start_flag = jnp.logical_or(position == 0, own_stream != prior_stream).astype(jnp.float32)
    keep = 1.0 - start_flag
    rim_query, rim_key, rim_value = from_behind(
        (query_feat[-2:], key_feat[-2:], values[-2:]), "seq", 1
    )
    qconv = convolve(query_feat, rim_query, conv_query, keep)
    kconv = convolve(key_feat, rim_key, conv_key, keep)
    vconv = convolve(values, rim_value, conv_value, keep)
    block = min(512, rows)
    nblocks = rows // block
    phq = taylor(qconv.reshape(rows, heads, FEAT).transpose(1, 0, 2).astype(jnp.float32)).astype(
        jnp.bfloat16
    )
    phk = taylor(kconv.reshape(rows, heads, FEAT).transpose(1, 0, 2).astype(jnp.float32)).astype(
        jnp.bfloat16
    )
    phq = phq.reshape(heads, nblocks, block, TAYLOR)
    phk = phk.reshape(heads, nblocks, block, TAYLOR)
    vblock = vconv.reshape(rows, heads, HD).transpose(1, 0, 2).reshape(heads, nblocks, block, HD)
    causal = jnp.tril(jnp.ones((block, block), jnp.float32))
    scores = (
        jnp.einsum("hbif,hbjf->hbij", phq, phk, preferred_element_type=jnp.float32) * causal
    ).astype(jnp.bfloat16)
    local = jnp.einsum("hbij,hbjd->hbid", scores, vblock, preferred_element_type=jnp.float32)
    kvsum = jnp.einsum("hbjf,hbjd->hbfd", phk, vblock, preferred_element_type=jnp.float32)
    running_sum = jnp.cumsum(kvsum, axis=1)
    earlier_blocks = jnp.concatenate([jnp.zeros_like(kvsum), running_sum[:, :-1]], axis=1)
    shard_total = running_sum[:, -1]
    identity = (jnp.zeros((), jnp.float32), jnp.zeros_like(shard_total))
    scanned = entering((start_flag, shard_total), "seq", segment_combine, identity)
    incoming = scanned[1] * keep
    states = incoming[:, None] + earlier_blocks
    carried = jnp.einsum(
        "hbif,hbfd->hbid", phq.astype(jnp.float32), states, precision=lax.Precision.HIGHEST
    )
    result = (local + carried).reshape(heads, rows, HD)
    gains = norm_gain.reshape(heads, HD)
    normed = (
        result
        * lax.rsqrt(jnp.mean(result * result, axis=-1, keepdims=True) + 1e-05)
        * gains[:, None, :]
    )
    hidden = normed.astype(jnp.bfloat16).transpose(1, 0, 2).reshape(rows, heads * HD)
    terms = jnp.dot(
        hidden,
        lax.all_gather(out_weight, "seq", axis=1, tiled=True),
        preferred_element_type=jnp.float32,
    )
    return lax.psum_scatter(terms.astype(jnp.bfloat16), "head", scatter_dimension=1, tiled=True)


def solution(mesh):
    placed = (
        P("seq", "head"),
        P("seq", "head"),
        P("seq", "head"),
        P(None, "head"),
        P(None, "head"),
        P(None, "head"),
        P("head"),
        P("head", "seq"),
        P(),
    )
    return jax.shard_map(
        on_device, mesh=mesh, in_specs=placed, out_specs=P("seq", "head"), check_vma=False
    )
```

profile of v0, /device:TPU:1, one launch (start us, length us, event | category | flops | bytes accessed | tf_op | source)
XLA Modules:
  0.0 432.2 jit_solution(11349278973005846561)
XLA Ops:
  7.3 4.6 %collective-permute-start = (bf16[2,64]{0,1:T(8,128)(2,1)S(1)}, bf16[2,64]{0,1:T(8,128)(2,1)S(1)}, u32[]{:S(2)}, u32[]{:S(2)}) collective-permute-start(bf16[2,64]{0,1:T(8,128)(2,1)S(1)} %slice.55), channel_id=1, source_target_pairs={{0,8},{8,16},{16,24},{24,32},{32,40},{40,48},{48,56},{56,64},{64,7... | collective-permute-start | bytes 776 | tf_op jit(solution)/shard_map/ppermute | solution.py:14
  12.7 1.9 collective-permute-start.1
  15.3 3.6 collective-permute-start.2
  31.6 127.6 %all-reduce = f32[64]{0:T(128)S(1)} all-reduce(f32[64]{0:T(128)S(1)} %dynamic-update-slice), channel_id=1, replica_groups=mesh['seq'=64,'head'=8] {'seq'}, use_global_device_ids=true, to_apply=%add | all-reduce | flops 64 | bytes 512
  159.6 4.5 %fusion.1 = f32[4,512,128]{1,2,0:T(8,128)} fusion(f32[512,512]{1,0:T(8,128)} %fusion.10, bf16[4,512,256]{1,2,0:T(8,128)(2,1)S(1)} %bitcast.66, bf16[4,512,16]{1,2,0:T(8,128)(2,1)S(1)} %convert.20, bf16[4,512,256]{1,2,0:T(8,128)(2,1)S(1)} %bitcast.67, bf16[4,512,16]{1,2,0:T(8,128)(2,1)S(1)} %bitcast_convert_fusion, bf16[273]{0:T(512)(128)(2,1)S(1)} %pad.7.clone, ...), kind=kOutput, calls=%fused_computation.6 | convolution fusion | flops 849764352 | bytes 4850210 | tf_op jit(solution)/shard_map/hbij,hbjd->hbid/dot_general | solution.py:92
  164.2 21.5 %all-gather.6.cloned.1.call-done = f32[256,273,128]{2,1,0:T(8,128)} async-done(((f32[4,273,128]{2,1,0:T(8,128)}), f32[256,273,128]{2,1,0:T(8,128)}) %all-gather.6.cloned.1.call-update) | async-done | bytes 35782672 | tf_op jit(solution)/shard_map/all_gather | solution.py:19
  185.7 176.0 %while.14 = (s32[]{:T(128)}, f32[4,273,128]{2,1,0:T(8,128)S(1)}, s32[]{:T(128)}, f32[64,4,273,128]{3,2,1,0:T(8,128)}, f32[64]{0:T(128)S(1)}, /*index=5*/s32[]{:T(128)}, f32[1]{0:T(128)}, s32[]{:T(128)}) while((s32[]{:T(128)}, f32[4,273,128]{2,1,0:T(8,128)S(1)}, s32[]{:T(128)}, f32[64,4,273,128]{3,2,1,0:T(8,128)}, f32[64]{0:T(128)S(1)}, ...), condition=%wide.region_1.2_spmd.clone, body=%wide.region_0.1_spmd.clone.sunk | while | flops 559109 | bytes 1677449 | solution.py:28
  186.9 1.5 fusion.42
  189.7 1.5 fusion.42
  192.5 1.5 fusion.42
  195.3 1.5 fusion.42
  198.1 1.5 fusion.42
  200.9 1.5 fusion.42
  203.7 1.5 fusion.42
  206.5 1.5 fusion.42
  209.2 1.5 fusion.42
  212.0 1.5 fusion.42
  214.8 1.5 fusion.42
  217.6 1.5 fusion.42
  220.4 1.5 fusion.42
  223.2 1.5 fusion.42
  226.0 1.5 fusion.42
  228.8 1.5 fusion.42
  231.6 1.5 fusion.42
  234.4 1.5 fusion.42
  237.2 1.5 fusion.42
  245.6 1.6 fusion.42
  251.2 1.6 fusion.42
  254.0 1.5 fusion.42
  259.6 1.6 fusion.42
  363.3 6.6 %convolution_convert_fusion = bf16[512,4096]{1,0:T(8,128)(2,1)} fusion(bf16[512,512]{0,1:T(8,128)(2,1)S(1)} %bitcast.69, bf16[512,4096]{0,1:T(8,128)(2,1)} %all-gather.4.cloned.1.call-done), kind=kOutput, calls=%fused_computation.2 | convolution fusion | flops 2149580800 | bytes 8912896 | tf_op jit(solution)/shard_map/dot_general | solution.py:112
  369.9 55.8 %reduce-scatter.2.cloned.1.call-done = bf16[512,512]{1,0:T(8,128)(2,1)} async-done(((bf16[512,4096]{1,0:T(8,128)(2,1)}), bf16[512,512]{1,0:T(8,128)(2,1)}) %reduce-scatter.2.cloned.1.call-update) | async-done | bytes 524304 | tf_op jit(solution)/shard_map/reduce_scatter | solution.py:117
  (150 shorter events, 116.0 us)
Async XLA Ops:
  6.5 179.1 %all-gather.6.cloned.1.call-start = ((), (), s32[]{:S(2)}) async-start(), calls=%async_computation.3 | async-start | bytes 37273600 | tf_op jit(solution)/shard_map/all_gather | solution.py:19
  7.3 17.9 %collective-permute-start = (bf16[2,64]{0,1:T(8,128)(2,1)S(1)}, bf16[2,64]{0,1:T(8,128)(2,1)S(1)}, u32[]{:S(2)}, u32[]{:S(2)}) collective-permute-start(bf16[2,64]{0,1:T(8,128)(2,1)S(1)} %slice.55), channel_id=1, source_target_pairs={{0,8},{8,16},{16,24},{24,32},{32,40},{40,48},{48,56},{56,64},{64,7... | collective-permute-start | bytes 776 | tf_op jit(solution)/shard_map/ppermute | solution.py:14
  12.7 12.5 %collective-permute-start.1 = (bf16[2,64]{0,1:T(8,128)(2,1)S(1)}, bf16[2,64]{0,1:T(8,128)(2,1)S(1)}, u32[]{:S(2)}, u32[]{:S(2)}) collective-permute-start(bf16[2,64]{0,1:T(8,128)(2,1)S(1)} %slice.61), channel_id=1, source_target_pairs={{0,8},{8,16},{16,24},{24,32},{32,40},{40,48},{48,56},{56,64},{64,7... | collective-permute-start | bytes 776 | tf_op jit(solution)/shard_map/ppermute | solution.py:14
  15.3 10.4 %collective-permute-start.2 = (bf16[2,512]{1,0:T(2,128)(2,1)S(1)}, bf16[2,512]{1,0:T(2,128)(2,1)S(1)}, u32[]{:S(2)}, u32[]{:S(2)}) collective-permute-start(bf16[2,512]{1,0:T(2,128)(2,1)S(1)} %slice.67), channel_id=1, source_target_pairs={{0,8},{8,16},{16,24},{24,32},{32,40},{40,48},{48,56},{56,64},{64,7... | collective-permute-start | bytes 6152 | tf_op jit(solution)/shard_map/ppermute | solution.py:14
  26.1 2.3 copy-start
  26.1 3.4 copy-start.2
  27.6 335.7 %all-gather.4.cloned.1.call-start = ((), (), s32[]{:S(2)}) async-start(), calls=%async_computation.1 | async-start | bytes 4259840 | tf_op jit(solution)/shard_map/all_gather | solution.py:114
  28.3 397.3 %reduce-scatter.2.cloned.1.call-start = ((), (), s32[]{:S(2)}) async-start(), calls=%async_computation.2 | async-start | bytes 4718592 | tf_op jit(solution)/shard_map/reduce_scatter | solution.py:117
  185.7 176.0 %copy-start.3 = (f32[4,512,128]{1,2,0:T(8,128)S(1)}, f32[4,512,128]{1,2,0:T(8,128)}, u32[]{:S(2)}) copy-start(f32[4,512,128]{1,2,0:T(8,128)} %fusion.1) | copy-start | bytes 3145732
  361.7 1.4 copy-start.1
Sparse Core Ops, SparseCore 0:
  27.7 157.9 all-gather.5
  189.0 81.7 all-gather.3
  370.0 55.6 reduce-scatter.1
where the time goes:
time: 436 us; the launch traced here: 432 us
  blocking collectives  128 us (29%)
  other arithmetic  102 us (23%)
  waiting for transfers between devices  78 us (18%)
  local copies, waits for them, and re-layouts  46.2 us (11%)
  loops' own time  40 us (9%)
  between operations  14.6 us (3%)
  matrix products  13.9 us (3%)
  starting transfers between devices  10.1 us (2%)
    unnamed x1, blocking collectives  128 us
    select_n x63, other arithmetic, lap(): jnp.where(position < mine, new, old)  97.2 us
    reduce_scatter x1, waiting for transfers between devices, on_device(): lax.psum_scatter(terms.astype(jnp.bfloat16), 'head', scatter_dimension=1,...  55.8 us
    another operation x1, loops' own time, entering(): return lax.fori_loop(0, count - 1, lap, so_far)  40 us
    dynamic_slice x63, local copies, waits for them, and re-layouts, lap(): longer = join(so_far, jax.tree.map(lambda part: part[position], pieces))  38.9 us
    all_gather x1, waiting for transfers between devices, entering(): pieces = jax.tree.map(lambda part: lax.all_gather(part, axis), value)  21.5 us
    ppermute x3, starting transfers between devices, from_behind(): return lax.ppermute(block, axis, route)  10.1 us
  transfers between devices with their start and end apart: 6, of which 2 were waited for; matrix products, arithmetic and copies ran while one was open for 35% of the time, Pallas kernels for 0%

commit v1 on v0

v1 whole, which is shorter than its diff:
```python
import numpy as np
import jax
import jax.numpy as jnp
from jax import lax
from jax.sharding import PartitionSpec as P

HD = 128
FEAT = 16
PAD = 160


def tables(heads):
    left = np.zeros((heads * FEAT, heads * PAD), np.float32)
    right = np.zeros((heads * FEAT, heads * PAD), np.float32)
    add_left = np.zeros((1, heads * PAD), np.float32)
    add_right = np.zeros((1, heads * PAD), np.float32)
    scale = np.zeros((1, heads * PAD), np.float32)
    twice = np.zeros((1, heads * PAD), np.float32)
    for h in range(heads):
        at = h * PAD
        add_left[0, at] = add_right[0, at] = scale[0, at] = twice[0, at] = 1.0
        for i in range(FEAT):
            at = h * PAD + 1 + i
            left[h * FEAT + i, at] = 1.0
            add_right[0, at] = scale[0, at] = twice[0, at] = 1.0
        at = h * PAD + 1 + FEAT
        for i in range(FEAT):
            for j in range(i, FEAT):
                left[h * FEAT + i, at] = 1.0
                right[h * FEAT + j, at] = 1.0
                scale[0, at] = np.float32(0.5**0.5)
                twice[0, at] = 1.0 if i == j else 2.0
                at += 1
    return left, right, add_left, add_right, scale, twice


def taylor(conv, heads):
    left, right, add_left, add_right, scale, twice = tables(heads)
    a = (conv.astype(jnp.float32) * FEAT ** (-0.25)).astype(jnp.bfloat16)
    one = jnp.dot(a, jnp.asarray(left, jnp.bfloat16), preferred_element_type=jnp.float32) + add_left
    two = jnp.dot(a, jnp.asarray(right, jnp.bfloat16), preferred_element_type=jnp.float32) + add_right
    return ((one * two) * scale).astype(jnp.bfloat16), jnp.asarray(twice, jnp.bfloat16)


def convolve(inputs, rim_rows, kernel, keep):
    padded = jnp.concatenate(
        [rim_rows.astype(jnp.float32) * keep, inputs.astype(jnp.float32)], axis=0
    )
    return (kernel[0] * padded[:-2] + kernel[1] * padded[1:-1] + kernel[2] * padded[2:]).astype(
        jnp.bfloat16
    )


def on_device(
    query_feat,
    key_feat,
    values,
    conv_query,
    conv_key,
    conv_value,
    norm_gain,
    out_weight,
    stream_ids,
):
    rows, qw = query_feat.shape
    heads = values.shape[1] // HD
    shards = lax.axis_size("seq")
    weight = lax.all_gather(out_weight.T, "seq", axis=0, tiled=True)
    position = lax.axis_index("seq")
    own_stream = stream_ids[position]
    prior_stream = stream_ids[jnp.maximum(position - 1, 0)]
    keep = 1.0 - jnp.logical_or(position == 0, own_stream != prior_stream).astype(jnp.float32)
    rim = jnp.concatenate([query_feat[-2:], key_feat[-2:], values[-2:]], axis=1)
    rim = lax.ppermute(rim, "seq", [(i, i + 1) for i in range(shards - 1)])
    qconv = convolve(query_feat, rim[:, :qw], conv_query, keep)
    kconv = convolve(key_feat, rim[:, qw : 2 * qw], conv_key, keep)
    vconv = convolve(values, rim[:, 2 * qw :], conv_value, keep)
    phk, twice = taylor(kconv, heads)
    kv = [
        lax.dot_general(
            phk[:, h * PAD : (h + 1) * PAD],
            vconv[:, h * HD : (h + 1) * HD],
            (((0,), (0,)), ((), ())),
            preferred_element_type=jnp.float32,
        )
        for h in range(heads)
    ]
    pieces = jnp.concatenate(kv, axis=0).astype(jnp.bfloat16).reshape(shards, -1, HD)
    pieces = lax.all_to_all(pieces, "seq", 0, 0, tiled=True)
    order = jnp.arange(shards)
    earlier = (stream_ids[:, None] == stream_ids[None, :]) & (order[None, :] < order[:, None])
    sums = jnp.einsum(
        "ds,skl->dkl", earlier.astype(jnp.bfloat16), pieces, preferred_element_type=jnp.float32
    ).astype(jnp.bfloat16)
    state = lax.all_to_all(sums, "seq", 0, 0, tiled=True).reshape(heads, PAD, HD)
    phq, _ = taylor(qconv, heads)
    phq = phq * twice
    causal = jnp.tril(jnp.ones((rows, rows), jnp.bool_))
    hidden = []
    for h in range(heads):
        q = phq[:, h * PAD : (h + 1) * PAD]
        k = phk[:, h * PAD : (h + 1) * PAD]
        v = vconv[:, h * HD : (h + 1) * HD]
        scores = lax.dot_general(
            q, k, (((1,), (1,)), ((), ())), preferred_element_type=jnp.float32
        )
        scores = jnp.where(causal, scores, 0.0).astype(jnp.bfloat16)
        y = jnp.dot(scores, v, preferred_element_type=jnp.float32) + jnp.dot(
            q, state[h], preferred_element_type=jnp.float32
        )
        gain = norm_gain[h * HD : (h + 1) * HD]
        y = y * lax.rsqrt(jnp.mean(y * y, axis=-1, keepdims=True) + 1e-05) * gain
        hidden.append(y.astype(jnp.bfloat16))
    hidden = jnp.concatenate(hidden, axis=1)
    terms = lax.dot_general(
        hidden, weight, (((1,), (1,)), ((), ())), preferred_element_type=jnp.float32
    )
    return lax.psum_scatter(terms.astype(jnp.bfloat16), "head", scatter_dimension=1, tiled=True)


def solution(mesh):
    placed = (
        P("seq", "head"),
        P("seq", "head"),
        P("seq", "head"),
        P(None, "head"),
        P(None, "head"),
        P(None, "head"),
        P("head"),
        P("head", "seq"),
        P(),
    )
    return jax.shard_map(
        on_device, mesh=mesh, in_specs=placed, out_specs=P("seq", "head"), check_vma=False
    )
```

time: 436 us -> 172 us (0.39)
  blocking collectives: 128 us -> 0 us
  other arithmetic: 102 us -> 3.95 us
  loops' own time: 40 us -> 0 us
  local copies, waits for them, and re-layouts: 46.2 us -> 8.47 us
  waiting for transfers between devices: 78 us -> 110 us
  starting transfers between devices: 10.1 us -> 19.9 us
    unnamed x1 -> x0, blocking collectives: 128 us -> none
    select_n x64 -> x0, other arithmetic: 98.3 us -> none  [the longest x63 97.2 us: lap(): jnp.where(position < mine, new, old)]
    another operation x1 -> x0, loops' own time: 40 us -> none  [entering(): return lax.fori_loop(0, count - 1, lap, so_far)]
    dynamic_slice x63 -> x0, local copies, waits for them, and re-layouts: 38.9 us -> none  [lap(): longer = join(so_far, jax.tree.map(lambda part: part[position], pieces))]
    all_to_all x0 -> x2, waiting for transfers between devices: none -> 21.3 us  [the longest x1 10.7 us: on_device(): lax.all_to_all(sums, 'seq', 0, 0, tiled=True).reshape(heads, PAD, HD)]
    all_to_all x0 -> x2, starting transfers between devices: none -> 15.3 us  [the longest x1 9.33 us: on_device(): pieces = lax.all_to_all(pieces, 'seq', 0, 0, tiled=True)]
    all_gather x2 -> x1, waiting for transfers between devices: 21.5 us -> 32.4 us  [on_device(): weight = lax.all_gather(out_weight.T, 'seq', axis=0, tiled=True)]
    ppermute x3 -> x1, starting transfers between devices: 10.1 us -> 4.58 us  [on_device(): rim = lax.ppermute(rim, 'seq', [(i, i + 1) for i in range(shards - 1)])]
  transfers between devices with their start and end apart: 6 -> 5, of which waited for: 2 -> 4; matrix products, arithmetic and copies ran while one was open for 35% -> 11% of each run, Pallas kernels for 0% -> 0%
where the time goes in v1:
time: 172 us; the launch traced here: 171 us
  waiting for transfers between devices  110 us (64%)
  starting transfers between devices  19.9 us (12%)
  between operations  15 us (9%)
  matrix products  13.1 us (8%)
  local copies, waits for them, and re-layouts  8.47 us (5%)
  other arithmetic  3.95 us (2%)
    reduce_scatter x1, waiting for transfers between devices, on_device(): lax.psum_scatter(terms.astype(jnp.bfloat16), 'head', scatter_dimension=1,...  55.9 us
    all_gather x1, waiting for transfers between devices, on_device(): weight = lax.all_gather(out_weight.T, 'seq', axis=0, tiled=True)  32.4 us
    all_to_all x1, waiting for transfers between devices, on_device(): lax.all_to_all(sums, 'seq', 0, 0, tiled=True).reshape(heads, PAD, HD)  10.7 us
    all_to_all x1, waiting for transfers between devices, on_device(): pieces = lax.all_to_all(pieces, 'seq', 0, 0, tiled=True)  10.6 us
    all_to_all x1, starting transfers between devices, on_device(): pieces = lax.all_to_all(pieces, 'seq', 0, 0, tiled=True)  9.33 us
    dot_general x1, matrix products, on_device(): lax.dot_general(hidden, weight, (((1,), (1,)), ((), ())), preferred_eleme...  6.57 us
    all_to_all x1, starting transfers between devices, on_device(): lax.all_to_all(sums, 'seq', 0, 0, tiled=True).reshape(heads, PAD, HD)  5.94 us
    ppermute x1, starting transfers between devices, on_device(): rim = lax.ppermute(rim, 'seq', [(i, i + 1) for i in range(shards - 1)])  4.58 us
  transfers between devices with their start and end apart: 5, of which 4 were waited for; matrix products, arithmetic and copies ran while one was open for 11% of the time, Pallas kernels for 0%

profile of v1, /device:TPU:1, one launch (start us, length us, event | category | flops | bytes accessed | tf_op | source)
XLA Modules:
  0.0 170.8 jit_solution(12257114810949976883)
XLA Ops:
  6.5 0.7 all-gather.2.cloned.1.call-update
  7.3 0.7 slice.138
  8.0 0.8 slice.136
  8.8 0.8 slice.137
  9.8 4.6 %collective-permute-start = (bf16[2,640]{1,0:T(2,128)(2,1)S(1)}, bf16[2,640]{1,0:T(2,128)(2,1)S(1)}, u32[]{:S(2)}, u32[]{:S(2)}) collective-permute-start(bf16[2,640]{1,0:T(2,128)(2,1)S(1)} %pad_maximum_fusion.4), channel_id=1, source_target_pairs={{0,8},{8,16},{16,24},{24,32},{32,40},{40,48},{48,56},{56,64},{64,7... | collective-permute-start | bytes 7688 | tf_op jit(solution)/shard_map/ppermute | solution.py:74
  14.4 0.8 slice_bitcast_fusion.5
  15.2 0.8 fusion.90
  16.0 0.8 fusion.89
  16.9 0.8 slice_bitcast_fusion.2
  17.7 0.8 convert_element_type.86
  18.5 0.9 convert_element_type.92
  19.4 1.2 convert_element_type.99
  20.5 0.7 fusion.91
  23.1 0.3 convolution_add_fusion.1
  23.4 0.3 fusion.19
  23.9 0.4 fusion.5
  25.2 0.3 convolution_convert_fusion.4
  25.6 0.8 convert_element_type.101
  26.4 9.3 %all-to-all-start = ((bf16[64,10,128]{2,1,0:T(8,128)(2,1)}), bf16[64,10,128]{2,1,0:T(8,128)(2,1)S(1)}, u32[]{:S(2)}, u32[]{:S(2)}) async-start(bf16[64,10,128]{2,1,0:T(8,128)(2,1)} %convert_element_type.101), calls=%async_computation | async-start | bytes 524288 | tf_op jit(solution)/shard_map/all_to_all | solution.py:89
  35.9 0.4 convolution_add_fusion.3
  36.2 0.4 fusion.10
  36.6 0.6 fusion.11
  37.2 0.6 fusion.12
  37.9 10.6 %all-to-all-done = bf16[64,10,128]{2,1,0:T(8,128)(2,1)S(1)} async-done(((bf16[64,10,128]{2,1,0:T(8,128)(2,1)}), bf16[64,10,128]{2,1,0:T(8,128)(2,1)S(1)}, u32[]{:S(2)}, u32[]{:S(2)}) %all-to-all-start) | async-done | bytes 163872 | tf_op jit(solution)/shard_map/all_to_all | solution.py:89
  48.7 0.8 copy.40
  49.5 5.9 %all-to-all-start.1 = ((bf16[64,10,128]{2,1,0:T(8,128)(2,1)}), bf16[64,10,128]{2,1,0:T(8,128)(2,1)S(1)}, u32[]{:S(2)}, u32[]{:S(2)}) async-start(bf16[64,10,128]{2,1,0:T(8,128)(2,1)} %copy.40), calls=%async_computation.1 | async-start | bytes 524288 | tf_op jit(solution)/shard_map/all_to_all | solution.py:95
  55.5 0.6 fusion.13
  56.1 0.6 fusion.14
  56.7 10.7 %all-to-all-done.1 = bf16[64,10,128]{2,1,0:T(8,128)(2,1)S(1)} async-done(((bf16[64,10,128]{2,1,0:T(8,128)(2,1)}), bf16[64,10,128]{2,1,0:T(8,128)(2,1)S(1)}, u32[]{:S(2)}, u32[]{:S(2)}) %all-to-all-start.1) | async-done | bytes 163872 | tf_op jit(solution)/shard_map/all_to_all | solution.py:95
  69.1 32.4 %all-gather.2.cloned.1.call-done = bf16[4096,512]{1,0:T(8,128)(2,1)} async-done(((bf16[64,512]{1,0:T(8,128)(2,1)}), bf16[4096,512]{1,0:T(8,128)(2,1)}) %all-gather.2.cloned.1.call-update) | async-done | bytes 4194320 | tf_op jit(solution)/shard_map/all_gather | solution.py:68
  101.5 6.6 %convolution_convert_fusion = bf16[512,4096]{1,0:T(8,128)(2,1)} fusion(bf16[4096,512]{1,0:T(8,128)(2,1)} %all-gather.2.cloned.1.call-done, bf16[512,128]{0,1:T(8,128)(2,1)S(1)} %get-tuple-element.34, bf16[512,128]{0,1:T(8,128)(2,1)S(1)} %get-tuple-element.35, bf16[512,128]{0,1:T(8,128)(2,1)S(1)} %get-tuple-element.36, bf16[512,128]{0,1:T(8,128)(2,1)S(1)} %get-tuple-element.37), kind=kOutput, calls=%fused_computation | convolution fusion | flops 2151677952 | bytes 8912896 | tf_op jit(solution)/shard_map/dot_general | solution.py:115
  108.1 55.9 %reduce-scatter.2.cloned.1.call-done = bf16[512,512]{1,0:T(8,128)(2,1)} async-done(((bf16[512,4096]{1,0:T(8,128)(2,1)}), bf16[512,512]{1,0:T(8,128)(2,1)}) %reduce-scatter.2.cloned.1.call-update) | async-done | bytes 524304 | tf_op jit(solution)/shard_map/reduce_scatter | solution.py:118
  (47 shorter events, 3.9 us)
Async XLA Ops:
  6.5 16.5 %copy-start.4 = (f32[640]{0:T(1024)S(1)}, f32[640]{0:T(1024)}, u32[]{:S(2)}) copy-start(f32[640]{0:T(1024)} %constant.49) | copy-start | bytes 7684
  6.5 16.5 %copy-start.1 = (bf16[64,640]{1,0:T(8,128)(2,1)S(1)}, bf16[64,640]{1,0:T(8,128)(2,1)}, u32[]{:S(2)}) copy-start(bf16[64,640]{1,0:T(8,128)(2,1)} %constant.43.clone) | copy-start | bytes 245764
  6.5 14.0 %copy-start.5 = (s32[64]{0:T(128)S(1)}, s32[64]{0:T(128)}, u32[]{:S(2)}) copy-start(s32[64]{0:T(128)} %param.28) | copy-start | bytes 772
  6.5 94.9 %all-gather.2.cloned.1.call-start = ((), (), s32[]{:S(2)}) async-start(), calls=%async_computation.3 | async-start | bytes 4259840 | tf_op jit(solution)/shard_map/all_gather | solution.py:68
  9.8 12.8 %collective-permute-start = (bf16[2,640]{1,0:T(2,128)(2,1)S(1)}, bf16[2,640]{1,0:T(2,128)(2,1)S(1)}, u32[]{:S(2)}, u32[]{:S(2)}) collective-permute-start(bf16[2,640]{1,0:T(2,128)(2,1)S(1)} %pad_maximum_fusion.4), channel_id=1, source_target_pairs={{0,8},{8,16},{16,24},{24,32},{32,40},{40,48},{48,56},{56,64},{64,7... | collective-permute-start | bytes 7688 | tf_op jit(solution)/shard_map/ppermute | solution.py:74
  23.1 0.9 copy-start
  23.1 0.9 copy-start.2
  23.1 0.9 copy-start.3
  25.6 10.7 %copy-start.6 = (bf16[640]{0:T(1024)(128)(2,1)S(1)}, bf16[640]{0:T(1024)(128)(2,1)}, u32[]{:S(2)}) copy-start(bf16[640]{0:T(1024)(128)(2,1)} %constant.52) | copy-start | bytes 3844
  26.4 22.1 %all-to-all-start = ((bf16[64,10,128]{2,1,0:T(8,128)(2,1)}), bf16[64,10,128]{2,1,0:T(8,128)(2,1)S(1)}, u32[]{:S(2)}, u32[]{:S(2)}) async-start(bf16[64,10,128]{2,1,0:T(8,128)(2,1)} %convert_element_type.101), calls=%async_computation | async-start | bytes 524288 | tf_op jit(solution)/shard_map/all_to_all | solution.py:89
  49.5 17.9 %all-to-all-start.1 = ((bf16[64,10,128]{2,1,0:T(8,128)(2,1)}), bf16[64,10,128]{2,1,0:T(8,128)(2,1)S(1)}, u32[]{:S(2)}, u32[]{:S(2)}) async-start(bf16[64,10,128]{2,1,0:T(8,128)(2,1)} %copy.40), calls=%async_computation.1 | async-start | bytes 524288 | tf_op jit(solution)/shard_map/all_to_all | solution.py:95
  55.5 108.5 %reduce-scatter.2.cloned.1.call-start = ((), (), s32[]{:S(2)}) async-start(), calls=%async_computation.4 | async-start | bytes 4718592 | tf_op jit(solution)/shard_map/reduce_scatter | solution.py:118
Sparse Core Ops, SparseCore 0:
  10.7 90.7 all-gather.1
  108.2 55.7 reduce-scatter.1

commit v2 on v1

--- a/solution.py
+++ b/solution.py
@@ -2,11 +2,292 @@
 import jax
 import jax.numpy as jnp
 from jax import lax
+from jax.experimental import pallas as pl
+from jax.experimental.pallas import tpu as pltpu
 from jax.sharding import PartitionSpec as P
 
 HD = 128
 FEAT = 16
 PAD = 160
+X, Y, C = 4, 8, 2
+SHARDS = X * Y * C
+Z = 8
+TILE = 16
+MESH = pl.DeviceIdType.MESH
+
+
+def remote(src, dst, send_sem, recv_sem, axis, target):
+    return pltpu.make_async_remote_copy(
+        src_ref=src,
+        dst_ref=dst,
+        send_sem=send_sem,
+        recv_sem=recv_sem,
+        device_id={axis: target},
+        device_id_type=MESH,
+    )
+
+
+def exchange_kernel(
+    ids,
+    pieces,
+    w_ref,
+    wout,
+    state,
+    inbox,
+    sums,
+    own_sem,
+    x_send,
+    x_recv,
+    y_send,
+    y_recv,
+    c_send,
+    c_recv,
+    one_send,
+    one_recv,
+    two_send,
+    two_recv,
+    local_sem,
+):
+    npieces = pieces.shape[0]
+    me = lax.axis_index("seq")
+    c = lax.rem(me, C)
+    y = lax.rem(me // C, Y)
+    x = me // (C * Y)
+
+    def at(xx, yy, cc):
+        return (lax.rem(xx + X, X) * Y + lax.rem(yy + Y, Y)) * C + cc
+
+    barrier = pltpu.get_barrier_semaphore()
+
+    @pl.loop(1, SHARDS)
+    def _(j):
+        pl.semaphore_signal(
+            barrier, inc=1, device_id={"seq": lax.rem(me + j, SHARDS)}, device_id_type=MESH
+        )
+
+    own = pltpu.make_async_copy(w_ref, wout.at[x, y, c], own_sem)
+    own.start()
+    pl.semaphore_wait(barrier, SHARDS - 1)
+
+    along_x = [
+        remote(w_ref, wout.at[x, y, c], x_send.at[k], x_recv.at[k], "seq", at(x + k + 1, y, c))
+        for k in range(X - 1)
+    ]
+    for copy in along_x:
+        copy.start()
+
+    @pl.loop(0, npieces)
+    def _(p):
+        @pl.when(p != me)
+        def _():
+            remote(pieces.at[p], inbox.at[me], one_send, one_recv, "seq", p).start()
+
+    handler = me < npieces
+
+    @pl.when(handler)
+    def _():
+        keep = pltpu.make_async_copy(pieces.at[me], inbox.at[me], local_sem)
+        keep.start()
+        keep.wait()
+
+    def group(yy, part=None):
+        yy = lax.rem(yy + Y, Y)
+        if part is None:
+            return wout.at[:, yy, c]
+        return wout.at[part * (X // 2) : (part + 1) * (X // 2), yy, c]
+
+    def hop(k, up):
+        part = None if k < 3 else (0 if up else 1)
+        ref = group(y - k if up else y + k, part)
+        return remote(
+            ref,
+            ref,
+            y_send.at[0 if up else 1, k],
+            y_recv.at[0 if up else 1, k],
+            "seq",
+            at(x, y + 1 if up else y - 1, c),
+        )
+
+    def across(j, yy):
+        ref = group(yy)
+        return remote(ref, ref, c_send.at[j], c_recv.at[j], "seq", at(x, y, 1 - c))
+
+    own.wait()
+    for copy in along_x:
+        copy.wait_recv()
+    hops = [(hop(k, True), hop(k, False)) for k in range(4)]
+    partner = [across(0, y)]
+    for copy in hops[0]:
+        copy.start()
+    partner[0].start()
+
+    @pl.when(handler)
+    def _():
+        pltpu.make_async_copy(
+            inbox.at[pl.ds(0, SHARDS - 1)], inbox.at[pl.ds(0, SHARDS - 1)], one_recv
+        ).wait()
+
+        def step(s, acc):
+            before = jnp.maximum(s - 1, 0)
+            same = jnp.where((s > 0) & (ids[s] == ids[before]), 1.0, 0.0)
+            acc = (acc + inbox[before].astype(jnp.float32)) * same
+            sums[s] = acc.astype(jnp.bfloat16)
+            return acc
+
+        lax.fori_loop(0, SHARDS, step, jnp.zeros(inbox.shape[1:], jnp.float32))
+
+        @pl.loop(0, SHARDS)
+        def _(s):
+            @pl.when(s != me)
+            def _():
+                remote(sums.at[s], state.at[me], two_send, two_recv, "seq", s).start()
+
+        keep = pltpu.make_async_copy(sums.at[me], state.at[me], local_sem)
+        keep.start()
+        keep.wait()
+
+    for k in range(3):
+        hops[k][0].wait_recv()
+        hops[k][1].wait_recv()
+        for copy in hops[k + 1]:
+            copy.start()
+        for j, yy in ((1 + 2 * k, y - 1 - k), (2 + 2 * k, y + 1 + k)):
+            partner.append(across(j, yy))
+            partner[-1].start()
+    hops[3][0].wait_recv()
+    hops[3][1].wait_recv()
+    partner.append(across(7, y + 4))
+    partner[-1].start()
+
+    def drain(count, sem):
+        pltpu.make_async_copy(
+            inbox.at[pl.ds(0, count)], inbox.at[pl.ds(0, count)], sem
+        ).wait()
+
+    @pl.when(handler)
+    def _():
+        drain(npieces - 1, two_recv)
+        drain(SHARDS - 1, two_send)
+        drain(npieces - 1, one_send)
+
+    @pl.when(jnp.logical_not(handler))
+    def _():
+        drain(npieces, two_recv)
+        drain(npieces, one_send)
+
+    for copy in along_x:
+        copy.wait_send()
+    for pair in hops:
+        for copy in pair:
+            copy.wait_send()
+    for copy in partner:
+        copy.wait()
+
+
+def exchange(ids, pieces, block):
+    dma = pltpu.SemaphoreType.DMA
+    vmem = pl.BlockSpec(memory_space=pltpu.VMEM)
+    return pl.pallas_call(
+        exchange_kernel,
+        out_shape=(
+            jax.ShapeDtypeStruct((X, Y, C) + block.shape, block.dtype),
+            jax.ShapeDtypeStruct(pieces.shape, pieces.dtype),
+        ),
+        in_specs=[pl.BlockSpec(memory_space=pltpu.SMEM), vmem, vmem],
+        out_specs=(vmem, vmem),
+        scratch_shapes=[
+            pltpu.VMEM((SHARDS,) + pieces.shape[1:], jnp.bfloat16),
+            pltpu.VMEM((SHARDS,) + pieces.shape[1:], jnp.bfloat16),
+            dma,
+            dma((X - 1,)),
+            dma((X - 1,)),
+            dma((2, 4)),
+            dma((2, 4)),
+            dma((Y,)),
+            dma((Y,)),
+            dma,
+            dma,
+            dma,
+            dma,
+            dma,
+        ],
+        compiler_params=pltpu.CompilerParams(
+            collective_id=0, has_side_effects=True, vmem_limit_bytes=24 << 20
+        ),
+    )(ids, pieces, block)
+
+
+def project_kernel(hidden, weight, out, outbox, inbox, send, recv):
+    z = lax.axis_index("head")
+    up, down = lax.rem(z + 1, Z), lax.rem(z + Z - 1, Z)
+    barrier = pltpu.get_barrier_semaphore()
+    for neighbour in (up, down):
+        pl.semaphore_signal(barrier, inc=1, device_id={"head": neighbour}, device_id_type=MESH)
+    rows, cols = out.shape
+    half_rows, half_cols = rows // 2, cols // 2
+
+    def term(k, way, part):
+        goal = lax.rem(z + 2 * Z - 1 - k, Z) if way == 0 else lax.rem(z + 1 + k, Z)
+        first = pl.multiple_of(goal * cols + way * half_cols, half_cols)
+        return lax.dot_general(
+            hidden[part * half_rows : (part + 1) * half_rows, :],
+            weight[pl.ds(first, half_cols), :],
+            (((1,), (1,)), ((), ())),
+            preferred_element_type=jnp.float32,
+        )
+
+    def copy(k, way, part):
+        return remote(
+            outbox.at[k, way, part],
+            inbox.at[k, way, part],
+            send.at[k, way, part],
+            recv.at[k, way, part],
+            "head",
+            up if way == 0 else down,
+        )
+
+    streams = [(way, part) for part in range(2) for way in range(2)]
+    for k in range(Z):
+        for way, part in streams:
+            total = term(k, way, part)
+            if k > 0:
+                copy(k - 1, way, part).wait_recv()
+                total = total + inbox[k - 1, way, part].astype(jnp.float32)
+            if k < Z - 1:
+                outbox[k, way, part] = total.astype(jnp.bfloat16)
+                if k == 0 and (way, part) == streams[0]:
+                    pl.semaphore_wait(barrier, 2)
+                copy(k, way, part).start()
+            else:
+                out[
+                    part * half_rows : (part + 1) * half_rows,
+                    way * half_cols : (way + 1) * half_cols,
+                ] = total.astype(jnp.bfloat16)
+    for k in range(Z - 1):
+        for way, part in streams:
+            copy(k, way, part).wait_send()
+
+
+def project(hidden, weight):
+    rows, cols = hidden.shape[0], weight.shape[0] // Z
+    dma = pltpu.SemaphoreType.DMA
+    vmem = pl.BlockSpec(memory_space=pltpu.VMEM)
+    boxes = (Z - 1, 2, 2, rows // 2, cols // 2)
+    return pl.pallas_call(
+        project_kernel,
+        out_shape=jax.ShapeDtypeStruct((rows, cols), jnp.bfloat16),
+        in_specs=[vmem, vmem],
+        out_specs=vmem,
+        scratch_shapes=[
+            pltpu.VMEM(boxes, jnp.bfloat16),
+            pltpu.VMEM(boxes, jnp.bfloat16),
+            dma((Z - 1, 2, 2)),
+            dma((Z - 1, 2, 2)),
+        ],
+        compiler_params=pltpu.CompilerParams(
+            collective_id=1, has_side_effects=True, vmem_limit_bytes=32 << 20
+        ),
+    )(hidden, weight)
 
 
 def tables(heads):
@@ -65,7 +346,6 @@
     rows, qw = query_feat.shape
     heads = values.shape[1] // HD
     shards = lax.axis_size("seq")
-    weight = lax.all_gather(out_weight.T, "seq", axis=0, tiled=True)
     position = lax.axis_index("seq")
     own_stream = stream_ids[position]
     prior_stream = stream_ids[jnp.maximum(position - 1, 0)]
@@ -85,14 +365,10 @@
         )
         for h in range(heads)
     ]
-    pieces = jnp.concatenate(kv, axis=0).astype(jnp.bfloat16).reshape(shards, -1, HD)
-    pieces = lax.all_to_all(pieces, "seq", 0, 0, tiled=True)
-    order = jnp.arange(shards)
-    earlier = (stream_ids[:, None] == stream_ids[None, :]) & (order[None, :] < order[:, None])
-    sums = jnp.einsum(
-        "ds,skl->dkl", earlier.astype(jnp.bfloat16), pieces, preferred_element_type=jnp.float32
-    ).astype(jnp.bfloat16)
-    state = lax.all_to_all(sums, "seq", 0, 0, tiled=True).reshape(heads, PAD, HD)
+    pieces = jnp.concatenate(kv, axis=0).astype(jnp.bfloat16).reshape(-1, TILE, HD)
+    weight, state = exchange(stream_ids, pieces, out_weight.T)
+    weight = weight.reshape(-1, weight.shape[-1])
+    state = state.reshape(heads, PAD, HD)
     phq, _ = taylor(qconv, heads)
     phq = phq * twice
     causal = jnp.tril(jnp.ones((rows, rows), jnp.bool_))
@@ -112,10 +388,7 @@
         y = y * lax.rsqrt(jnp.mean(y * y, axis=-1, keepdims=True) + 1e-05) * gain
         hidden.append(y.astype(jnp.bfloat16))
     hidden = jnp.concatenate(hidden, axis=1)
-    terms = lax.dot_general(
-        hidden, weight, (((1,), (1,)), ((), ())), preferred_element_type=jnp.float32
-    )
-    return lax.psum_scatter(terms.astype(jnp.bfloat16), "head", scatter_dimension=1, tiled=True)
+    return project(hidden, weight)
 
 
 def solution(mesh):

time: 172 us -> 127 us (0.74)
  waiting for transfers between devices: 110 us -> 0.01 us
  Pallas kernels: 0 us -> 101 us
  starting transfers between devices: 19.9 us -> 4.58 us
  between operations: 15 us -> 1.59 us
  matrix products: 13.1 us -> 6.71 us
    pallas_call x0 -> x2, Pallas kernels: none -> 101 us  [the longest x1 51.5 us: exchange(): pl.pallas_call(exchange_kernel, out_shape=(jax.ShapeDtypeStruct((X, Y, C)...]
    reduce_scatter x1 -> x0, waiting for transfers between devices: 55.9 us -> none  [on_device(): lax.psum_scatter(terms.astype(jnp.bfloat16), 'head', scatter_dimension=1,...]
    all_gather x1 -> x0, waiting for transfers between devices: 32.4 us -> none  [on_device(): weight = lax.all_gather(out_weight.T, 'seq', axis=0, tiled=True)]
    all_to_all x2 -> x0, waiting for transfers between devices: 21.3 us -> none  [the longest x1 10.7 us: on_device(): lax.all_to_all(sums, 'seq', 0, 0, tiled=True).reshape(heads, PAD, HD)]
    all_to_all x2 -> x0, starting transfers between devices: 15.3 us -> none  [the longest x1 9.33 us: on_device(): pieces = lax.all_to_all(pieces, 'seq', 0, 0, tiled=True)]
    dot_general x2 -> x0, matrix products: 6.82 us -> none  [the longest x1 6.57 us: on_device(): lax.dot_general(hidden, weight, (((1,), (1,)), ((), ())), preferred_eleme...]
  transfers between devices with their start and end apart: 5 -> 1, of which waited for: 4 -> 0; matrix products, arithmetic and copies ran while one was open for 11% -> 5% of each run, Pallas kernels for 0% -> 0%
where the time goes in v2:
time: 127 us; the launch traced here: 126 us
  Pallas kernels  101 us (80%)
  local copies, waits for them, and re-layouts  7.7 us (6%)
  matrix products  6.71 us (5%)
  starting transfers between devices  4.58 us (4%)
  other arithmetic  4.26 us (3%)
  between operations  1.59 us (1%)
    pallas_call x1, Pallas kernels, exchange(): pl.pallas_call(exchange_kernel, out_shape=(jax.ShapeDtypeStruct((X, Y, C)...  51.5 us
    pallas_call x1, Pallas kernels, project(): pl.pallas_call(project_kernel, out_shape=jax.ShapeDtypeStruct((rows, cols...  49.8 us
    ppermute x1, starting transfers between devices, on_device(): rim = lax.ppermute(rim, 'seq', [(i, i + 1) for i in range(shards - 1)])  4.58 us
    convert_element_type x3, other arithmetic, convolve(): inputs.astype(jnp.float32)  2.89 us
  transfers between devices with their start and end apart: 1, of which 0 were waited for; matrix products, arithmetic and copies ran while one was open for 5% of the time, Pallas kernels for 0%

profile of v2, /device:TPU:1, one launch (start us, length us, event | category | flops | bytes accessed | tf_op | source)
XLA Modules:
  0.0 126.1 jit_solution(15008811167231172514)
XLA Ops:
  0.0 0.7 slice.138
  0.8 0.8 slice.136
  1.6 0.8 slice.137
  2.6 4.6 %collective-permute-start = (bf16[2,640]{1,0:T(2,128)(2,1)S(1)}, bf16[2,640]{1,0:T(2,128)(2,1)S(1)}, u32[]{:S(2)}, u32[]{:S(2)}) collective-permute-start(bf16[2,640]{1,0:T(2,128)(2,1)S(1)} %pad_maximum_fusion.5), channel_id=1, source_target_pairs={{0,8},{8,16},{16,24},{24,32},{32,40},{40,48},{48,56},{56,64},{64,7... | collective-permute-start | bytes 7688 | tf_op jit(solution)/shard_map/ppermute | solution.py:354
  7.2 0.8 slice_bitcast_fusion.5
  8.0 0.8 fusion.75
  8.8 0.8 fusion.74
  9.6 0.8 slice_bitcast_fusion.2
  10.4 0.8 convert_element_type.79
  11.3 0.9 convert_element_type.85
  12.2 1.2 convert_element_type.92
  13.4 0.7 fusion.76
  15.7 0.4 convolution_add_fusion.1
  16.1 0.4 fusion.5
  16.5 0.3 fusion.19
  17.1 0.3 convolution_convert_fusion
  17.4 0.3 convolution_convert_fusion.1
  17.8 0.3 convolution_convert_fusion.2
  18.4 0.3 convolution_add_fusion.3
  18.7 0.4 fusion.10
  19.1 0.6 fusion.11
  19.8 0.6 fusion.12
  20.4 0.6 fusion.13
  21.1 0.6 fusion.14
  21.7 0.2 copy-done
  21.9 51.5 %shard_map.190 = (bf16[4,8,2,64,512]{4,3,2,1,0:T(8,128)(2,1)S(1)}, bf16[40,16,128]{2,1,0:T(8,128)(2,1)S(1)}) custom-call(s32[64]{0:T(128)S(1)} %copy-done.1, bf16[40,16,128]{2,1,0:T(8,128)(2,1)S(1)} %bitcast.36, bf16[64,512]{1,0:T(8,128)(2,1)S(1)} %bitcast.37), custom_call_target="tpu_custom_call" | custom-call | tf_op jit(solution)/shard_map/pallas_call | solution.py:190
  73.5 0.3 multiply_reduce_fusion.3
  73.8 0.4 multiply_reduce_fusion
  74.2 0.4 multiply_reduce_fusion.2
  74.6 0.4 multiply_reduce_fusion.1
  75.5 49.8 %shard_map.191 = bf16[512,512]{1,0:T(8,128)(2,1)S(1)} custom-call(bf16[512,512]{1,0:T(8,128)(2,1)S(1)} %pad_maximum_fusion.1.hidden, bf16[4096,512]{1,0:T(8,128)(2,1)S(1)} %bitcast.35), custom_call_target="tpu_custom_call" | custom-call | tf_op jit(solution)/shard_map/pallas_call | solution.py:276
  125.3 0.8 copy.44
  (35 shorter events, 1.7 us)
Async XLA Ops:
  0.0 15.7 %copy-start.6 = (f32[640]{0:T(1024)S(1)}, f32[640]{0:T(1024)}, u32[]{:S(2)}) copy-start(f32[640]{0:T(1024)} %constant.49) | copy-start | bytes 7684
  0.0 15.7 %copy-start.3 = (bf16[64,640]{1,0:T(8,128)(2,1)S(1)}, bf16[64,640]{1,0:T(8,128)(2,1)}, u32[]{:S(2)}) copy-start(bf16[64,640]{1,0:T(8,128)(2,1)} %constant.43.clone) | copy-start | bytes 245764
  0.0 13.4 %copy-start.1 = (s32[64]{0:T(128)S(1)}, s32[64]{0:T(128)}, u32[]{:S(2)}) copy-start(s32[64]{0:T(128)} %ids.1) | copy-start | bytes 772
  2.6 12.7 %collective-permute-start = (bf16[2,640]{1,0:T(2,128)(2,1)S(1)}, bf16[2,640]{1,0:T(2,128)(2,1)S(1)}, u32[]{:S(2)}, u32[]{:S(2)}) collective-permute-start(bf16[2,640]{1,0:T(2,128)(2,1)S(1)} %pad_maximum_fusion.5), channel_id=1, source_target_pairs={{0,8},{8,16},{16,24},{24,32},{32,40},{40,48},{48,56},{56,64},{64,7... | collective-permute-start | bytes 7688 | tf_op jit(solution)/shard_map/ppermute | solution.py:354
  12.2 3.9 %copy-start.2 = (bf16[64,640]{1,0:T(8,128)(2,1)S(1)}, bf16[64,640]{1,0:T(8,128)(2,1)}, u32[]{:S(2)}) copy-start(bf16[64,640]{1,0:T(8,128)(2,1)} %constant.45.clone) | copy-start | bytes 245764
  12.2 3.9 %copy-start.4 = (f32[640]{0:T(1024)S(1)}, f32[640]{0:T(1024)}, u32[]{:S(2)}) copy-start(f32[640]{0:T(1024)} %constant.51) | copy-start | bytes 7684
  12.2 3.9 %copy-start.5 = (f32[640]{0:T(1024)S(1)}, f32[640]{0:T(1024)}, u32[]{:S(2)}) copy-start(f32[640]{0:T(1024)} %constant.50) | copy-start | bytes 7684
  17.4 1.3 %copy-start.7 = (bf16[640]{0:T(1024)(128)(2,1)S(1)}, bf16[640]{0:T(1024)(128)(2,1)}, u32[]{:S(2)}) copy-start(bf16[640]{0:T(1024)(128)(2,1)} %constant.52) | copy-start | bytes 3844
  21.1 0.8 copy-start

commit v3 on v2

v3 whole, which is shorter than its diff:
```python
import numpy as np
import jax
import jax.numpy as jnp
from jax import lax
from jax.experimental import pallas as pl
from jax.experimental.pallas import tpu as pltpu
from jax.sharding import PartitionSpec as P

HD = 128
FEAT = 16
PAD = 160
X, Y, C = 4, 8, 2
SHARDS = X * Y * C
Z = 8
TILE = 16
MESH = pl.DeviceIdType.MESH


def remote(src, dst, send_sem, recv_sem, axis, target):
    return pltpu.make_async_remote_copy(
        src_ref=src,
        dst_ref=dst,
        send_sem=send_sem,
        recv_sem=recv_sem,
        device_id={axis: target},
        device_id_type=MESH,
    )


def shifted(x, rim, axis):
    where = lax.broadcasted_iota(jnp.int32, x.shape, axis)
    far, near = lax.slice_in_dim(rim, 0, 1, axis=axis), lax.slice_in_dim(rim, 1, 2, axis=axis)
    one = jnp.where(where == 0, near, pltpu.roll(x, 1, axis))
    two = jnp.where(where == 0, far, jnp.where(where == 1, near, pltpu.roll(x, 2, axis)))
    return one, two


def exchange_kernel(
    ids,
    q_in,
    k_in,
    v_in,
    cq,
    ck,
    cv,
    gain,
    w_ref,
    q_left,
    q_right,
    q_scale,
    k_left,
    k_right,
    k_scale,
    wout,
    hidden,
    q_rim,
    k_rim,
    v_rim,
    phk,
    phq,
    vconv,
    local,
    pieces,
    state,
    inbox,
    sums,
    rim_send,
    rim_recv,
    own_sem,
    x_send,
    x_recv,
    y_send,
    y_recv,
    c_send,
    c_recv,
    one_send,
    one_recv,
    two_send,
    two_recv,
    local_sem,
):
    npieces = pieces.shape[0]
    heads = phq.shape[0]
    rows = v_in.shape[0]
    per_head = npieces // heads
    me = lax.axis_index("seq")
    c = lax.rem(me, C)
    y = lax.rem(me // C, Y)
    x = me // (C * Y)

    def at(xx, yy, cc):
        return (lax.rem(xx + X, X) * Y + lax.rem(yy + Y, Y)) * C + cc

    barrier = pltpu.get_barrier_semaphore()

    @pl.loop(1, SHARDS)
    def _(j):
        pl.semaphore_signal(
            barrier, inc=1, device_id={"seq": lax.rem(me + j, SHARDS)}, device_id_type=MESH
        )

    own = pltpu.make_async_copy(w_ref, wout.at[x, y, c], own_sem)
    own.start()
    pl.semaphore_wait(barrier, SHARDS - 1)

    after = lax.rem(me + 1, SHARDS)
    edges = (
        (q_in.at[:, pl.ds(rows - 128, 128)], q_rim),
        (k_in.at[:, pl.ds(rows - 128, 128)], k_rim),
        (v_in.at[pl.ds(rows - TILE, TILE), :], v_rim),
    )
    rims = [
        remote(src, dst, rim_send.at[i], rim_recv.at[i], "seq", after)
        for i, (src, dst) in enumerate(edges)
    ]
    for copy in rims:
        copy.start()
    along_x = [
        remote(w_ref, wout.at[x, y, c], x_send.at[k], x_recv.at[k], "seq", at(x + k + 1, y, c))
        for k in range(X - 1)
    ]
    for copy in along_x:
        copy.start()

    handler = me < npieces

    def group(yy, part=None):
        yy = lax.rem(yy + Y, Y)
        if part is None:
            return wout.at[:, yy, c]
        return wout.at[part * (X // 2) : (part + 1) * (X // 2), yy, c]

    def hop(k, way, part):
        ref = group(y - k if way == 0 else y + k, part)
        return remote(
            ref,
            ref,
            y_send.at[way, k, part],
            y_recv.at[way, k, part],
            "seq",
            at(x, y + 1 if way == 0 else y - 1, c),
        )

    hops = []

    def launch(k):
        for part in range(2):
            for way in range(2):
                if k > 0:
                    hop(k - 1, way, part).wait_recv()
                if k < 3 or way == part:
                    hops.append(hop(k, way, part))
                    hops[-1].start()

    def across(j, yy):
        ref = group(yy)
        return remote(ref, ref, c_send.at[j], c_recv.at[j], "seq", at(x, y, 1 - c))

    keep = jnp.where((me > 0) & (ids[me] == ids[jnp.maximum(me - 1, 0)]), 1.0, 0.0)
    wide_ones = jnp.ones((TILE, rows), jnp.bfloat16)

    def features_in(src, rim, taps, axis_keep):
        past = rim[...].astype(jnp.float32)[:, 126:128] * axis_keep
        now = src[...].astype(jnp.float32)
        one, two = shifted(now, past, 1)
        conv = taps[:, 0:1] * two + taps[:, 1:2] * one + taps[:, 2:3] * now
        conv = conv.astype(jnp.bfloat16).astype(jnp.float32)
        return jnp.concatenate([(conv * FEAT ** (-0.25)).astype(jnp.bfloat16), wide_ones], axis=0)

    own.wait()
    for copy in rims:
        copy.wait_recv()
    k_a = features_in(k_in, k_rim, ck, keep)
    for h in range(heads):
        span = slice(h * PAD, (h + 1) * PAD)
        one = jnp.dot(k_left[span, :], k_a, preferred_element_type=jnp.float32)
        two = jnp.dot(k_right[span, :], k_a, preferred_element_type=jnp.float32)
        phk[h] = ((one * two) * k_scale[span, :]).astype(jnp.bfloat16)
        lanes = slice(h * HD, (h + 1) * HD)
        now = v_in[:, lanes].astype(jnp.float32)
        past = v_rim[:, lanes].astype(jnp.float32)[TILE - 2 : TILE, :] * keep
        one, two = shifted(now, past, 0)
        conv = cv[0:1, lanes] * two + cv[1:2, lanes] * one + cv[2:3, lanes] * now
        vconv[:, lanes] = conv.astype(jnp.bfloat16)
        kv = jnp.dot(phk[h], vconv[:, lanes], preferred_element_type=jnp.float32)
        pieces[h * per_head : (h + 1) * per_head] = kv.astype(jnp.bfloat16).reshape(
            per_head, TILE, HD
        )

    @pl.loop(0, npieces)
    def _(p):
        @pl.when(p != me)
        def _():
            remote(pieces.at[p], inbox.at[me], one_send, one_recv, "seq", p).start()

    @pl.when(handler)
    def _():
        mine = pltpu.make_async_copy(pieces.at[me], inbox.at[me], local_sem)
        mine.start()
        mine.wait()

    for copy in along_x:
        copy.wait_recv()
    launch(0)
    partner = [across(0, y)]
    partner[0].start()

    q_a = features_in(q_in, q_rim, cq, keep)

    def attend(h):
        turn = (((0,), (0,)), ((), ()))
        one = lax.dot_general(q_a, q_left[h], turn, preferred_element_type=jnp.float32)
        two = lax.dot_general(q_a, q_right[h], turn, preferred_element_type=jnp.float32)
        phq[h] = ((one * two) * q_scale[...]).astype(jnp.bfloat16)
        scores = jnp.dot(phq[h], phk[h], preferred_element_type=jnp.float32)
        i = lax.broadcasted_iota(jnp.int32, scores.shape, 0)
        j = lax.broadcasted_iota(jnp.int32, scores.shape, 1)
        scores = jnp.where(j <= i, scores, 0.0).astype(jnp.bfloat16)
        lanes = slice(h * HD, (h + 1) * HD)
        local[:, lanes] = jnp.dot(scores, vconv[:, lanes], preferred_element_type=jnp.float32)

    def relay(k):
        launch(k + 1)
        for j, yy in ((1 + 2 * k, y - 1 - k), (2 + 2 * k, y + 1 + k)):
            partner.append(across(j, yy))
            partner[-1].start()

    attend(0)
    attend(1)

    @pl.when(handler)
    def _():
        pltpu.make_async_copy(
            inbox.at[pl.ds(0, SHARDS - 1)], inbox.at[pl.ds(0, SHARDS - 1)], one_recv
        ).wait()

        def step(s, acc):
            before = jnp.maximum(s - 1, 0)
            same = jnp.where((s > 0) & (ids[s] == ids[before]), 1.0, 0.0)
            acc = (acc + inbox[before].astype(jnp.float32)) * same
            sums[s] = acc.astype(jnp.bfloat16)
            return acc

        lax.fori_loop(0, SHARDS, step, jnp.zeros(inbox.shape[1:], jnp.float32))

        @pl.loop(0, SHARDS)
        def _(s):
            @pl.when(s != me)
            def _():
                remote(sums.at[s], state.at[me], two_send, two_recv, "seq", s).start()

        mine = pltpu.make_async_copy(sums.at[me], state.at[me], local_sem)
        mine.start()
        mine.wait()

    relay(0)
    attend(2)
    attend(3)
    relay(1)

    def drain(count, sem):
        pltpu.make_async_copy(
            inbox.at[pl.ds(0, count)], inbox.at[pl.ds(0, count)], sem
        ).wait()

    @pl.when(handler)
    def _():
        drain(npieces - 1, two_recv)
        drain(SHARDS - 1, two_send)
        drain(npieces - 1, one_send)

    @pl.when(jnp.logical_not(handler))
    def _():
        drain(npieces, two_recv)
        drain(npieces, one_send)

    for h in range(heads):
        lanes = slice(h * HD, (h + 1) * HD)
        mine = state[h * per_head : (h + 1) * per_head].reshape(PAD, HD)
        total = local[:, lanes] + jnp.dot(phq[h], mine, preferred_element_type=jnp.float32)
        power = jnp.mean(total * total, axis=-1, keepdims=True)
        hidden[:, lanes] = (total * lax.rsqrt(power + 1e-05) * gain[:, lanes]).astype(jnp.bfloat16)

    relay(2)
    hop(3, 0, 0).wait_recv()
    hop(3, 1, 1).wait_recv()
    partner.append(across(7, y + 4))
    partner[-1].start()

    for copy in rims + along_x + hops:
        copy.wait_send()
    for copy in partner:
        copy.wait()


def exchange(ids, q, k, v, cq, ck, cv, gain, block, *constants):
    dma = pltpu.SemaphoreType.DMA
    vmem = pl.BlockSpec(memory_space=pltpu.VMEM)
    rows, wide = v.shape
    heads = wide // HD
    narrow = q.shape[0]
    npieces = heads * PAD // TILE
    half = jnp.bfloat16
    return pl.pallas_call(
        exchange_kernel,
        out_shape=(
            jax.ShapeDtypeStruct((X, Y, C) + block.shape, block.dtype),
            jax.ShapeDtypeStruct(v.shape, half),
        ),
        in_specs=[pl.BlockSpec(memory_space=pltpu.SMEM)] + [vmem] * (8 + len(constants)),
        out_specs=(vmem, vmem),
        scratch_shapes=[
            pltpu.VMEM((narrow, 128), half),
            pltpu.VMEM((narrow, 128), half),
            pltpu.VMEM((TILE, wide), half),
            pltpu.VMEM((heads, PAD, rows), half),
            pltpu.VMEM((heads, rows, PAD), half),
            pltpu.VMEM((rows, wide), half),
            pltpu.VMEM((rows, wide), jnp.float32),
            pltpu.VMEM((npieces, TILE, HD), half),
            pltpu.VMEM((npieces, TILE, HD), half),
            pltpu.VMEM((SHARDS, TILE, HD), half),
            pltpu.VMEM((SHARDS, TILE, HD), half),
            dma((3,)),
            dma((3,)),
            dma,
            dma((X - 1,)),
            dma((X - 1,)),
            dma((2, 4, 2)),
            dma((2, 4, 2)),
            dma((Y,)),
            dma((Y,)),
            dma,
            dma,
            dma,
            dma,
            dma,
        ],
        compiler_params=pltpu.CompilerParams(
            collective_id=0, has_side_effects=True, vmem_limit_bytes=40 << 20
        ),
    )(ids, q, k, v, cq, ck, cv, gain, block, *constants)


def project_kernel(hidden, weight, out, outbox, inbox, send, recv):
    z = lax.axis_index("head")
    up, down = lax.rem(z + 1, Z), lax.rem(z + Z - 1, Z)
    barrier = pltpu.get_barrier_semaphore()
    for neighbour in (up, down):
        pl.semaphore_signal(barrier, inc=1, device_id={"head": neighbour}, device_id_type=MESH)
    rows, cols = out.shape
    half_rows, half_cols = rows // 2, cols // 2

    def term(k, way, part):
        goal = lax.rem(z + 2 * Z - 1 - k, Z) if way == 0 else lax.rem(z + 1 + k, Z)
        first = pl.multiple_of(goal * cols + way * half_cols, half_cols)
        return lax.dot_general(
            hidden[part * half_rows : (part + 1) * half_rows, :],
            weight[pl.ds(first, half_cols), :],
            (((1,), (1,)), ((), ())),
            preferred_element_type=jnp.float32,
        )

    def copy(k, way, part):
        return remote(
            outbox.at[k, way, part],
            inbox.at[k, way, part],
            send.at[k, way, part],
            recv.at[k, way, part],
            "head",
            up if way == 0 else down,
        )

    streams = [(way, part) for part in range(2) for way in range(2)]
    for k in range(Z):
        for way, part in streams:
            total = term(k, way, part)
            if k > 0:
                copy(k - 1, way, part).wait_recv()
                total = total + inbox[k - 1, way, part].astype(jnp.float32)
            if k < Z - 1:
                outbox[k, way, part] = total.astype(jnp.bfloat16)
                if k == 0 and (way, part) == streams[0]:
                    pl.semaphore_wait(barrier, 2)
                copy(k, way, part).start()
            else:
                out[
                    part * half_rows : (part + 1) * half_rows,
                    way * half_cols : (way + 1) * half_cols,
                ] = total.astype(jnp.bfloat16)
    for k in range(Z - 1):
        for way, part in streams:
            copy(k, way, part).wait_send()


def project(hidden, weight):
    rows, cols = hidden.shape[0], weight.shape[0] // Z
    dma = pltpu.SemaphoreType.DMA
    vmem = pl.BlockSpec(memory_space=pltpu.VMEM)
    boxes = (Z - 1, 2, 2, rows // 2, cols // 2)
    return pl.pallas_call(
        project_kernel,
        out_shape=jax.ShapeDtypeStruct((rows, cols), jnp.bfloat16),
        in_specs=[vmem, vmem],
        out_specs=vmem,
        scratch_shapes=[
            pltpu.VMEM(boxes, jnp.bfloat16),
            pltpu.VMEM(boxes, jnp.bfloat16),
            dma((Z - 1, 2, 2)),
            dma((Z - 1, 2, 2)),
        ],
        compiler_params=pltpu.CompilerParams(
            collective_id=1, has_side_effects=True, vmem_limit_bytes=32 << 20
        ),
    )(hidden, weight)


def tables(heads):
    wide = heads * FEAT + TILE
    bias = heads * FEAT
    left = np.zeros((heads, PAD, wide), np.float32)
    right = np.zeros((heads, PAD, wide), np.float32)
    scale = np.zeros((PAD,), np.float32)
    twice = np.ones((PAD,), np.float32)
    scale[: 1 + FEAT] = 1.0
    left[:, 0, bias] = 1.0
    right[:, : 1 + FEAT, bias] = 1.0
    for h in range(heads):
        at = 1 + FEAT
        for i in range(FEAT):
            left[h, 1 + i, h * FEAT + i] = 1.0
            for j in range(i, FEAT):
                left[h, at, h * FEAT + i] = 1.0
                right[h, at, h * FEAT + j] = 1.0
                scale[at] = np.float32(0.5**0.5)
                twice[at] = 1.0 if i == j else 2.0
                at += 1
    flat = (heads * PAD, wide)
    return (
        jnp.asarray(left.transpose(0, 2, 1), jnp.bfloat16),
        jnp.asarray(right.transpose(0, 2, 1), jnp.bfloat16),
        jnp.asarray((scale * twice)[None, :]),
        jnp.asarray(left.reshape(flat), jnp.bfloat16),
        jnp.asarray(right.reshape(flat), jnp.bfloat16),
        jnp.asarray(np.tile(scale, heads)[:, None]),
    )


def on_device(
    query_feat,
    key_feat,
    values,
    conv_query,
    conv_key,
    conv_value,
    norm_gain,
    out_weight,
    stream_ids,
):
    heads = values.shape[1] // HD
    weight, hidden = exchange(
        stream_ids,
        query_feat.T,
        key_feat.T,
        values,
        conv_query.T,
        conv_key.T,
        conv_value,
        norm_gain[None, :],
        out_weight.T,
        *tables(heads),
    )
    return project(hidden, weight.reshape(-1, weight.shape[-1]))


def solution(mesh):
    placed = (
        P("seq", "head"),
        P("seq", "head"),
        P("seq", "head"),
        P(None, "head"),
        P(None, "head"),
        P(None, "head"),
        P("head"),
        P("head", "seq"),
        P(),
    )
    return jax.shard_map(
        on_device, mesh=mesh, in_specs=placed, out_specs=P("seq", "head"), check_vma=False
    )
```

time: 127 us -> 114 us (0.90)
  matrix products: 6.71 us -> 0 us
  local copies, waits for them, and re-layouts: 7.7 us -> 13.2 us
  starting transfers between devices: 4.58 us -> 0 us
  other arithmetic: 4.26 us -> 0 us
  between operations: 1.59 us -> 0.03 us
    unnamed x19 -> x29, local copies, waits for them, and re-layouts: 1.25 us -> 13.2 us
    dot_general x16 -> x0, matrix products: 6.71 us -> none  [the longest x4 2.48 us: on_device(): jnp.dot(scores, v, preferred_element_type=jnp.float32)]
    ppermute x1 -> x0, starting transfers between devices: 4.58 us -> none  [on_device(): rim = lax.ppermute(rim, 'seq', [(i, i + 1) for i in range(shards - 1)])]
    slice x6 -> x0, local copies, waits for them, and re-layouts: 4.01 us -> none  [the longest x3 2.35 us: on_device(): rim = jnp.concatenate([query_feat[-2:], key_feat[-2:], values[-2:]], axis=1)]
    convert_element_type x8 -> x0, other arithmetic: 4 us -> none  [the longest x3 2.89 us: convolve(): inputs.astype(jnp.float32)]
    pallas_call x1, Pallas kernels: 51.5 us -> 49.5 us  [exchange(): pl.pallas_call(exchange_kernel, out_shape=(jax.ShapeDtypeStruct((X, Y, C)...]
    mul x4 -> x0, local copies, waits for them, and re-layouts: 1.79 us -> none  [the longest x2 1.59 us: convolve(): kernel[0] * padded[:-2] + kernel[1] * padded[1:-1] + kernel[2] * padded[2:]]
  transfers between devices with their start and end apart: 1 -> 0, of which waited for: 0 -> 0; matrix products, arithmetic and copies ran while one was open for 5% -> 0% of each run, Pallas kernels for 0% -> 0%
where the time goes in v3:
time: 114 us
  Pallas kernels  100 us (88%)
  local copies, waits for them, and re-layouts  13.2 us (12%)
    pallas_call x1, Pallas kernels, project(): pl.pallas_call(project_kernel, out_shape=jax.ShapeDtypeStruct((rows, cols...  50.8 us
    pallas_call x1, Pallas kernels, exchange(): pl.pallas_call(exchange_kernel, out_shape=(jax.ShapeDtypeStruct((X, Y, C)...  49.5 us
    unnamed x29, local copies, waits for them, and re-layouts  13.2 us

profile of v3, /device:TPU:1, one launch (start us, length us, event | category | flops | bytes accessed | tf_op | source)
XLA Modules:
  0.0 113.6 jit_solution(10894307739851226268)
XLA Ops:
  0.0 0.8 copy.16
  0.8 0.8 copy.17
  1.5 0.0 copy-start
  1.5 1.0 copy-done
  2.6 0.0 copy-start.1
  2.6 1.0 copy-done.1
  3.6 0.0 copy-start.2
  3.6 0.9 copy-done.2
  4.5 0.0 copy-start.3
  4.5 0.9 copy-done.3
  5.4 0.0 copy-start.4
  5.4 0.9 copy-done.4
  6.3 0.0 copy-start.5
  6.3 0.9 copy-done.5
  7.2 0.0 copy-start.6
  7.2 0.8 copy-done.6
  8.1 0.0 copy-start.7
  8.1 0.8 copy-done.7
  8.9 0.0 copy-start.8
  8.9 0.8 copy-done.8
  9.7 0.0 copy-start.9
  9.7 0.7 copy-done.9
  10.4 0.0 copy-start.10
  10.4 0.7 copy-done.10
  11.1 0.0 copy-start.11
  11.1 0.7 copy-done.11
  11.8 0.0 copy-start.12
  11.8 0.7 copy-done.12
  12.5 49.5 %shard_map.145 = (bf16[4,8,2,64,512]{4,3,2,1,0:T(8,128)(2,1)S(1)}, bf16[512,512]{1,0:T(8,128)(2,1)S(1)}) custom-call(s32[64]{0:T(128)S(1)} %copy-done.12, bf16[64,512]{1,0:T(8,128)(2,1)S(1)} %bitcast.10, bf16[64,512]{1,0:T(8,128)(2,1)S(1)} %bitcast.11, bf16[512,512]{1,0:T(8,128)(2,1)S(1)} %copy-done, f32[64,3]{1,0:T(8,128)S(1)} %bitcast.8, ...), custom_call_target="tpu_custom_call" | custom-call | tf_op jit(solution)/shard_map/pallas_call | solution.py:304
  62.0 50.8 %shard_map.146 = bf16[512,512]{1,0:T(8,128)(2,1)S(1)} custom-call(bf16[512,512]{1,0:T(8,128)(2,1)S(1)} %get-tuple-element.7.hidden, bf16[4096,512]{1,0:T(8,128)(2,1)S(1)} %bitcast.7), custom_call_target="tpu_custom_call" | custom-call | tf_op jit(solution)/shard_map/pallas_call | solution.py:401
  112.8 0.8 copy.19
Async XLA Ops:
  1.5 1.0 copy-start
  2.6 1.0 copy-start.1
  3.6 0.9 copy-start.2
  4.5 0.9 copy-start.3
  5.4 0.9 copy-start.4
  6.3 0.9 copy-start.5
  7.2 0.8 copy-start.6
  8.1 0.8 copy-start.7
  8.9 0.8 copy-start.8
  9.7 0.7 copy-start.9
  10.4 0.7 copy-start.10
  11.1 0.7 copy-start.11
  11.8 0.7 copy-start.12

commit v4 on v3

--- a/solution.py
+++ b/solution.py
@@ -13,6 +13,7 @@
 SHARDS = X * Y * C
 Z = 8
 TILE = 16
+NSCRATCH = 36
 MESH = pl.DeviceIdType.MESH
 
 
@@ -35,24 +36,26 @@
     return one, two
 
 
-def exchange_kernel(
+def layer_kernel(
     ids,
-    q_in,
-    k_in,
-    v_in,
-    cq,
-    ck,
-    cv,
-    gain,
+    *refs,
+):
+    count = (len(refs) - NSCRATCH) // 2
+    w_ref, far, out = refs[0], refs[1:count], refs[count]
+    near = refs[count + 1 : 2 * count]
+    scratch = refs[2 * count :]
+    mix_body(ids, w_ref, far, near, *scratch[:-4])
+    project_body(scratch[1], scratch[0], out, *scratch[-4:])
+
+
+def mix_body(
+    ids,
     w_ref,
-    q_left,
-    q_right,
-    q_scale,
-    k_left,
-    k_right,
-    k_scale,
+    far,
+    near,
     wout,
     hidden,
+    in_sem,
     q_rim,
     k_rim,
     v_rim,
@@ -71,6 +74,10 @@
     x_recv,
     y_send,
     y_recv,
+    b_send,
+    b_recv,
+    bx_send,
+    bx_recv,
     c_send,
     c_recv,
     one_send,
@@ -79,6 +86,11 @@
     two_recv,
     local_sem,
 ):
+    fetches = [pltpu.make_async_copy(a, b, in_sem.at[i]) for i, (a, b) in enumerate(zip(far, near))]
+    for copy in fetches:
+        copy.start()
+    (q_in, k_in, v_in, cq, ck, cv, gain) = near[:7]
+    (q_left, q_right, q_scale, k_left, k_right, k_scale) = near[7:]
     npieces = pieces.shape[0]
     heads = phq.shape[0]
     rows = v_in.shape[0]
@@ -99,9 +111,12 @@
             barrier, inc=1, device_id={"seq": lax.rem(me + j, SHARDS)}, device_id_type=MESH
         )
 
+    z = lax.axis_index("head")
+    for neighbour in (lax.rem(z + 1, Z), lax.rem(z + Z - 1, Z)):
+        pl.semaphore_signal(barrier, inc=1, device_id={"head": neighbour}, device_id_type=MESH)
     own = pltpu.make_async_copy(w_ref, wout.at[x, y, c], own_sem)
     own.start()
-    pl.semaphore_wait(barrier, SHARDS - 1)
+    pl.semaphore_wait(barrier, SHARDS + 1)
 
     after = lax.rem(me + 1, SHARDS)
     edges = (
@@ -113,13 +128,24 @@
         remote(src, dst, rim_send.at[i], rim_recv.at[i], "seq", after)
         for i, (src, dst) in enumerate(edges)
     ]
+    for copy in fetches[:3]:
+        copy.wait()
     for copy in rims:
         copy.start()
+    half = wout.shape[3] // 2
+    top, low = pl.ds(0, half), pl.ds(half, half)
+    own.wait()
+
+    def spread(k, ref, send, recv, target):
+        return remote(ref, ref, send.at[k], recv.at[k], "seq", target)
+
     along_x = [
-        remote(w_ref, wout.at[x, y, c], x_send.at[k], x_recv.at[k], "seq", at(x + k + 1, y, c))
-        for k in range(X - 1)
+        spread(k, wout.at[x, y, c, top], x_send, x_recv, at(x + k + 1, y, c)) for k in range(X - 1)
     ]
-    for copy in along_x:
+    along_y = [
+        spread(k, wout.at[x, y, c, low], b_send, b_recv, at(x, y + k + 1, c)) for k in range(Y - 1)
+    ]
+    for copy in along_x + along_y:
         copy.start()
 
     handler = me < npieces
@@ -127,34 +153,44 @@
     def group(yy, part=None):
         yy = lax.rem(yy + Y, Y)
         if part is None:
-            return wout.at[:, yy, c]
-        return wout.at[part * (X // 2) : (part + 1) * (X // 2), yy, c]
-
-    def hop(k, way, part):
-        ref = group(y - k if way == 0 else y + k, part)
-        return remote(
-            ref,
-            ref,
-            y_send.at[way, k, part],
-            y_recv.at[way, k, part],
-            "seq",
-            at(x, y + 1 if way == 0 else y - 1, c),
-        )
+            return wout.at[:, yy, c, top]
+        return wout.at[part * (X // 2) : (part + 1) * (X // 2), yy, c, top]
+
+    def column(xx, part=None):
+        xx = lax.rem(xx + X, X)
+        if part is None:
+            return wout.at[xx, :, c, low]
+        return wout.at[xx, part * (Y // 2) : (part + 1) * (Y // 2), c, low]
+
+    def hop(k, way):
+        ref = group(y - k if way == 0 else y + k, None if k < 3 else way)
+        goal = at(x, y + 1 if way == 0 else y - 1, c)
+        return remote(ref, ref, y_send.at[way, k], y_recv.at[way, k], "seq", goal)
+
+    def leap(k, way):
+        ref = column(x - k if way == 0 else x + k, None if k < 1 else way)
+        goal = at(x + 1 if way == 0 else x - 1, y, c)
+        return remote(ref, ref, bx_send.at[way, k], bx_recv.at[way, k], "seq", goal)
 
     hops = []
-
-    def launch(k):
-        for part in range(2):
-            for way in range(2):
-                if k > 0:
-                    hop(k - 1, way, part).wait_recv()
-                if k < 3 or way == part:
-                    hops.append(hop(k, way, part))
-                    hops[-1].start()
-
-    def across(j, yy):
-        ref = group(yy)
-        return remote(ref, ref, c_send.at[j], c_recv.at[j], "seq", at(x, y, 1 - c))
+    partner = []
+
+    def launch(kind, k):
+        for way in range(2):
+            if k > 0:
+                kind(k - 1, way).wait_recv()
+        for way in range(2):
+            hops.append(kind(k, way))
+            hops[-1].start()
+
+    def across(j, ref):
+        partner.append(remote(ref, ref, c_send.at[j], c_recv.at[j], "seq", at(x, y, 1 - c)))
+        partner[-1].start()
+
+    def relay(k):
+        launch(hop, k + 1)
+        across(1 + 2 * k, group(y - 1 - k))
+        across(2 + 2 * k, group(y + 1 + k))
 
     keep = jnp.where((me > 0) & (ids[me] == ids[jnp.maximum(me - 1, 0)]), 1.0, 0.0)
     wide_ones = jnp.ones((TILE, rows), jnp.bfloat16)
@@ -167,7 +203,8 @@
         conv = conv.astype(jnp.bfloat16).astype(jnp.float32)
         return jnp.concatenate([(conv * FEAT ** (-0.25)).astype(jnp.bfloat16), wide_ones], axis=0)
 
-    own.wait()
+    for copy in fetches[3:]:
+        copy.wait()
     for copy in rims:
         copy.wait_recv()
     k_a = features_in(k_in, k_rim, ck, keep)
@@ -186,6 +223,11 @@
         pieces[h * per_head : (h + 1) * per_head] = kv.astype(jnp.bfloat16).reshape(
             per_head, TILE, HD
         )
+        if h == heads // 2 - 1:
+            for copy in along_x:
+                copy.wait_recv()
+            launch(hop, 0)
+            across(0, group(y))
 
     @pl.loop(0, npieces)
     def _(p):
@@ -199,11 +241,10 @@
         mine.start()
         mine.wait()
 
-    for copy in along_x:
+    for copy in along_y:
         copy.wait_recv()
-    launch(0)
-    partner = [across(0, y)]
-    partner[0].start()
+    launch(leap, 0)
+    across(8, column(x))
 
     q_a = features_in(q_in, q_rim, cq, keep)
 
@@ -219,13 +260,8 @@
         lanes = slice(h * HD, (h + 1) * HD)
         local[:, lanes] = jnp.dot(scores, vconv[:, lanes], preferred_element_type=jnp.float32)
 
-    def relay(k):
-        launch(k + 1)
-        for j, yy in ((1 + 2 * k, y - 1 - k), (2 + 2 * k, y + 1 + k)):
-            partner.append(across(j, yy))
-            partner[-1].start()
-
     attend(0)
+    relay(0)
     attend(1)
 
     @pl.when(handler)
@@ -253,10 +289,19 @@
         mine.start()
         mine.wait()
 
-    relay(0)
+    relay(1)
+    launch(leap, 1)
+    across(9, column(x - 1))
+    across(10, column(x + 1))
     attend(2)
+    relay(2)
     attend(3)
-    relay(1)
+    leap(1, 0).wait_recv()
+    leap(1, 1).wait_recv()
+    across(11, column(x + 2))
+    hop(3, 0).wait_recv()
+    hop(3, 1).wait_recv()
+    across(7, group(y + 4))
 
     def drain(count, sem):
         pltpu.make_async_copy(
@@ -281,19 +326,13 @@
         power = jnp.mean(total * total, axis=-1, keepdims=True)
         hidden[:, lanes] = (total * lax.rsqrt(power + 1e-05) * gain[:, lanes]).astype(jnp.bfloat16)
 
-    relay(2)
-    hop(3, 0, 0).wait_recv()
-    hop(3, 1, 1).wait_recv()
-    partner.append(across(7, y + 4))
-    partner[-1].start()
-
-    for copy in rims + along_x + hops:
+    for copy in rims + along_x + along_y + hops:
         copy.wait_send()
     for copy in partner:
         copy.wait()
 
 
-def exchange(ids, q, k, v, cq, ck, cv, gain, block, *constants):
+def layer(ids, q, k, v, cq, ck, cv, gain, block, *constants):
     dma = pltpu.SemaphoreType.DMA
     vmem = pl.BlockSpec(memory_space=pltpu.VMEM)
     rows, wide = v.shape
@@ -301,15 +340,19 @@
     narrow = q.shape[0]
     npieces = heads * PAD // TILE
     half = jnp.bfloat16
+    boxes = (Z - 1, 2, 2, rows // 2, SHARDS * block.shape[0] // Z // 2)
+    inputs = (q, k, v, cq, ck, cv, gain) + constants
     return pl.pallas_call(
-        exchange_kernel,
-        out_shape=(
-            jax.ShapeDtypeStruct((X, Y, C) + block.shape, block.dtype),
-            jax.ShapeDtypeStruct(v.shape, half),
-        ),
-        in_specs=[pl.BlockSpec(memory_space=pltpu.SMEM)] + [vmem] * (8 + len(constants)),
-        out_specs=(vmem, vmem),
-        scratch_shapes=[
+        layer_kernel,
+        out_shape=jax.ShapeDtypeStruct((rows, SHARDS * block.shape[0] // Z), half),
+        in_specs=[pl.BlockSpec(memory_space=pltpu.SMEM)]
+        + [pl.BlockSpec(memory_space=pltpu.HBM)] * (1 + len(inputs)),
+        out_specs=vmem,
+        scratch_shapes=[pltpu.VMEM(a.shape, a.dtype) for a in inputs]
+        + [
+            pltpu.VMEM((X, Y, C) + block.shape, half),
+            pltpu.VMEM(v.shape, half),
+            dma((len(inputs),)),
             pltpu.VMEM((narrow, 128), half),
             pltpu.VMEM((narrow, 128), half),
             pltpu.VMEM((TILE, wide), half),
@@ -326,37 +369,43 @@
             dma,
             dma((X - 1,)),
             dma((X - 1,)),
-            dma((2, 4, 2)),
-            dma((2, 4, 2)),
-            dma((Y,)),
-            dma((Y,)),
+            dma((2, 4)),
+            dma((2, 4)),
+            dma((Y - 1,)),
+            dma((Y - 1,)),
+            dma((2, 2)),
+            dma((2, 2)),
+            dma((X + Y,)),
+            dma((X + Y,)),
             dma,
             dma,
             dma,
             dma,
             dma,
+            pltpu.VMEM(boxes, half),
+            pltpu.VMEM(boxes, half),
+            dma(boxes[:3]),
+            dma(boxes[:3]),
         ],
         compiler_params=pltpu.CompilerParams(
-            collective_id=0, has_side_effects=True, vmem_limit_bytes=40 << 20
+            collective_id=0, has_side_effects=True, vmem_limit_bytes=60 << 20
         ),
-    )(ids, q, k, v, cq, ck, cv, gain, block, *constants)
-
-
-def project_kernel(hidden, weight, out, outbox, inbox, send, recv):
+    )(ids, block, *inputs)
+
+
+def project_body(hidden, wout, out, outbox, inbox, send, recv):
     z = lax.axis_index("head")
     up, down = lax.rem(z + 1, Z), lax.rem(z + Z - 1, Z)
-    barrier = pltpu.get_barrier_semaphore()
-    for neighbour in (up, down):
-        pl.semaphore_signal(barrier, inc=1, device_id={"head": neighbour}, device_id_type=MESH)
     rows, cols = out.shape
     half_rows, half_cols = rows // 2, cols // 2
 
     def term(k, way, part):
         goal = lax.rem(z + 2 * Z - 1 - k, Z) if way == 0 else lax.rem(z + 1 + k, Z)
-        first = pl.multiple_of(goal * cols + way * half_cols, half_cols)
+        first = goal * (SHARDS // Z) + way * (SHARDS // Z // 2)
+        weight = wout[first // (Y * C), pl.ds(lax.rem(first // C, Y), SHARDS // Z // 2 // C)]
         return lax.dot_general(
             hidden[part * half_rows : (part + 1) * half_rows, :],
-            weight[pl.ds(first, half_cols), :],
+            weight.reshape(half_cols, weight.shape[-1]),
             (((1,), (1,)), ((), ())),
             preferred_element_type=jnp.float32,
         )
@@ -380,8 +429,6 @@
                 total = total + inbox[k - 1, way, part].astype(jnp.float32)
             if k < Z - 1:
                 outbox[k, way, part] = total.astype(jnp.bfloat16)
-                if k == 0 and (way, part) == streams[0]:
-                    pl.semaphore_wait(barrier, 2)
                 copy(k, way, part).start()
             else:
                 out[
@@ -391,28 +438,6 @@
     for k in range(Z - 1):
         for way, part in streams:
             copy(k, way, part).wait_send()
-
-
-def project(hidden, weight):
-    rows, cols = hidden.shape[0], weight.shape[0] // Z
-    dma = pltpu.SemaphoreType.DMA
-    vmem = pl.BlockSpec(memory_space=pltpu.VMEM)
-    boxes = (Z - 1, 2, 2, rows // 2, cols // 2)
-    return pl.pallas_call(
-        project_kernel,
-        out_shape=jax.ShapeDtypeStruct((rows, cols), jnp.bfloat16),
-        in_specs=[vmem, vmem],
-        out_specs=vmem,
-        scratch_shapes=[
-            pltpu.VMEM(boxes, jnp.bfloat16),
-            pltpu.VMEM(boxes, jnp.bfloat16),
-            dma((Z - 1, 2, 2)),
-            dma((Z - 1, 2, 2)),
-        ],
-        compiler_params=pltpu.CompilerParams(
-            collective_id=1, has_side_effects=True, vmem_limit_bytes=32 << 20
-        ),
-    )(hidden, weight)
 
 
 def tables(heads):
@@ -458,7 +483,7 @@
     stream_ids,
 ):
     heads = values.shape[1] // HD
-    weight, hidden = exchange(
+    return layer(
         stream_ids,
         query_feat.T,
         key_feat.T,
@@ -470,7 +495,6 @@
         out_weight.T,
         *tables(heads),
     )
-    return project(hidden, weight.reshape(-1, weight.shape[-1]))
 
 
 def solution(mesh):

time: 114 us -> 98.2 us (0.86)
  local copies, waits for them, and re-layouts: 13.2 us -> 3.96 us
  Pallas kernels: 100 us -> 94.1 us
    unnamed x29 -> x7, local copies, waits for them, and re-layouts: 13.2 us -> 3.96 us
    pallas_call x2 -> x1, Pallas kernels: 100 us -> 94.1 us  [layer(): pl.pallas_call(layer_kernel, out_shape=jax.ShapeDtypeStruct((rows, SHARDS...]
where the time goes in v4:
time: 98.2 us; the launch traced here: 98 us
  Pallas kernels  94.1 us (96%)
  local copies, waits for them, and re-layouts  3.96 us (4%)
    pallas_call x1, Pallas kernels, layer(): pl.pallas_call(layer_kernel, out_shape=jax.ShapeDtypeStruct((rows, SHARDS...  94.1 us
    unnamed x7, local copies, waits for them, and re-layouts  3.96 us

profile of v4, /device:TPU:1, one launch (start us, length us, event | category | flops | bytes accessed | tf_op | source)
XLA Modules:
  0.0 98.0 jit_solution(1506224389017066138)
XLA Ops:
  0.0 0.0 copy-start
  0.0 0.7 copy-done
  0.7 0.0 copy-start.1
  0.7 0.7 copy.16
  1.4 0.0 copy-done.1
  1.4 0.7 copy.17
  2.1 94.1 %shard_map.145 = bf16[512,512]{1,0:T(8,128)(2,1)} custom-call(s32[64]{0:T(128)} %ids.1, bf16[64,512]{1,0:T(8,128)(2,1)} %bitcast.8, bf16[64,512]{1,0:T(8,128)(2,1)} %bitcast.9, bf16[64,512]{1,0:T(8,128)(2,1)} %bitcast.10, bf16[512,512]{1,0:T(8,128)(2,1)} %refs_3_.1, f32[64,3]{1,0:T(8,128)} %bitcast.6, f32[64,3]{1,0:T(8,128)} %bitcast.7, f32[3,512]{1,0:T(4,128)} %refs_6_.1, ...), custom_call_target="tpu_custom_call" | custom-call | tf_op jit(solution)/shard_map/pallas_call | solution.py:345
  96.2 1.9 %copy.19 = bf16[512,512]{1,0:T(8,128)(2,1)} copy(bf16[512,512]{1,0:T(8,128)(2,1)} %shard_map.145) | data formatting | bytes 1048576
Async XLA Ops:
  0.0 0.7 copy-start
  0.7 0.7 copy-start.1

commit v5 on v4

--- a/solution.py
+++ b/solution.py
@@ -199,7 +199,8 @@
         past = rim[...].astype(jnp.float32)[:, 126:128] * axis_keep
         now = src[...].astype(jnp.float32)
         one, two = shifted(now, past, 1)
-        conv = taps[:, 0:1] * two + taps[:, 1:2] * one + taps[:, 2:3] * now
+        turned = jnp.transpose(taps[...])
+        conv = turned[:, 0:1] * two + turned[:, 1:2] * one + turned[:, 2:3] * now
         conv = conv.astype(jnp.bfloat16).astype(jnp.float32)
         return jnp.concatenate([(conv * FEAT ** (-0.25)).astype(jnp.bfloat16), wide_ones], axis=0)
 
@@ -223,11 +224,6 @@
         pieces[h * per_head : (h + 1) * per_head] = kv.astype(jnp.bfloat16).reshape(
             per_head, TILE, HD
         )
-        if h == heads // 2 - 1:
-            for copy in along_x:
-                copy.wait_recv()
-            launch(hop, 0)
-            across(0, group(y))
 
     @pl.loop(0, npieces)
     def _(p):
@@ -241,6 +237,10 @@
         mine.start()
         mine.wait()
 
+    for copy in along_x:
+        copy.wait_recv()
+    launch(hop, 0)
+    across(0, group(y))
     for copy in along_y:
         copy.wait_recv()
     launch(leap, 0)
@@ -488,8 +488,8 @@
         query_feat.T,
         key_feat.T,
         values,
-        conv_query.T,
-        conv_key.T,
+        conv_query,
+        conv_key,
         conv_value,
         norm_gain[None, :],
         out_weight.T,

time: 98.2 us -> 99.1 us (level)
  Pallas kernels: 94.1 us -> 97.1 us
  local copies, waits for them, and re-layouts: 3.96 us -> 1.87 us
    pallas_call x1, Pallas kernels: 94.1 us -> 97.1 us  [layer(): pl.pallas_call(layer_kernel, out_shape=jax.ShapeDtypeStruct((rows, SHARDS...]
    unnamed x7 -> x1, local copies, waits for them, and re-layouts: 3.96 us -> 1.87 us
where the time goes in v5:
time: 99.1 us; the launch traced here: 99 us
  Pallas kernels  97.1 us (98%)
  local copies, waits for them, and re-layouts  1.87 us (2%)
    pallas_call x1, Pallas kernels, layer(): pl.pallas_call(layer_kernel, out_shape=jax.ShapeDtypeStruct((rows, SHARDS...  97.1 us

profile of v5, /device:TPU:1, one launch (start us, length us, event | category | flops | bytes accessed | tf_op | source)
XLA Modules:
  0.0 99.0 jit_solution(15388434180400293461)
XLA Ops:
  0.0 97.1 %shard_map.145 = bf16[512,512]{1,0:T(8,128)(2,1)} custom-call(s32[64]{0:T(128)} %ids.1, bf16[64,512]{1,0:T(8,128)(2,1)} %bitcast.4, bf16[64,512]{1,0:T(8,128)(2,1)} %bitcast.5, bf16[64,512]{1,0:T(8,128)(2,1)} %bitcast.6, bf16[512,512]{1,0:T(8,128)(2,1)} %refs_3_.1, f32[3,64]{1,0:T(4,128)} %refs_4_.1, f32[3,64]{1,0:T(4,128)} %refs_5_.1, f32[3,512]{1,0:T(4,128)} %refs_6_.1, ...), custom_call_target="tpu_custom_call" | custom-call | tf_op jit(solution)/shard_map/pallas_call | solution.py:345
  97.1 1.9 %copy.17 = bf16[512,512]{1,0:T(8,128)(2,1)} copy(bf16[512,512]{1,0:T(8,128)(2,1)} %shard_map.145) | data formatting | bytes 1048576
